TPU v7x, 32 devices: a whole 2x2x4 slice. The times are simulated.
32 devices in a mesh: blk: 8 (over y, x, core), ma: 4 (over z).
Axes of the slice: x: 2, y: 2, z: 4, core: 2. Of those that a mesh axis runs over, the one named last changes fastest.
Arguments:
- sky_map: float32 [2, 256, 65536], P(None, ('blk', 'ma')), may hold values from -6 to 6
- legendre: bfloat16 [256, 64, 4096], P(('blk', 'ma')), as said below
- m_list: int32 [4, 16], replicated, may hold values from 0 to 32767, as said below
- block_start: int32 [64, 64], replicated, may hold values from 0 to 511, as said below
- beam_ratio: float32 [32768], replicated, may hold values from 0.5 to 2
Outputs:
- harmonics: float32 [2, 64, 4096], P(None, 'ma', 'blk')
- spectrum: float32 [4096], P('blk')
Inputs may be any that keep to these rules, and one draw needn't show every extreme that they name: `m_list`: entries are distinct and equal one common offset plus multiples of 512. `block_start`: each row lists 64 distinct block numbers in increasing order. legendre[g, k, j] is zero wherever 64 * block_start[k, j // 64] + j mod 64 is below the k-th order of the flattened m_list.
All inputs are finite; a program needn't handle non-finite values.
Results may differ from a plain program's by a relative error of at most 0.0029.
Values may be sent and summed in bfloat16 or wider, within the bound.
A program may use at most 128 MiB of HBM per device.

v0:
```python
import math

import jax
import jax.numpy as jnp
from jax import lax
from jax.sharding import PartitionSpec as P

LBLK = 64


def cycle_fourier(sky, m_values, parity):
    hemispheres, cycle_rows, pixel_count = sky.shape
    flat_cycles = sky.reshape(hemispheres * cycle_rows, pixel_count)
    block_width = min(pixel_count, 8192)

    def add_block(running, block_index):
        segment = lax.dynamic_slice_in_dim(flat_cycles, block_index * block_width, block_width, 1)
        pixels = block_index * block_width + jnp.arange(block_width, dtype=jnp.int32)
        phase_turns = pixels[:, None] * m_values[None, :] % pixel_count
        angles = phase_turns.astype(jnp.float32) * (2.0 * math.pi / pixel_count)
        real_acc = running[0] + jnp.dot(
            segment,
            jnp.cos(angles),
            precision=lax.Precision.HIGHEST,
            preferred_element_type=jnp.float32,
        )
        imag_acc = running[1] - jnp.dot(
            segment,
            jnp.sin(angles),
            precision=lax.Precision.HIGHEST,
            preferred_element_type=jnp.float32,
        )
        return ((real_acc, imag_acc), block_index)

    empty_acc = jnp.zeros((hemispheres * cycle_rows, m_values.shape[0]), jnp.float32)
    sums, unused = lax.scan(
        add_block, (empty_acc, empty_acc), jnp.arange(pixel_count // block_width, dtype=jnp.int32)
    )
    normalizer = 1.0 / math.sqrt(pixel_count)
    real_part = sums[0].reshape(hemispheres, cycle_rows, -1) * normalizer
    imag_part = sums[1].reshape(hemispheres, cycle_rows, -1) * normalizer
    twist = (parity[:, None] * m_values[None, :]).astype(jnp.float32) * (math.pi / pixel_count)
    cos_twist = jnp.cos(twist)
    sin_twist = jnp.sin(twist)
    rot_real = real_part * cos_twist + imag_part * sin_twist
    rot_imag = imag_part * cos_twist - real_part * sin_twist
    folded = jnp.stack(
        [
            rot_real[0] + rot_real[1],
            rot_imag[0] + rot_imag[1],
            rot_real[0] - rot_real[1],
            rot_imag[0] - rot_imag[1],
        ]
    )
    return folded.astype(jnp.bfloat16)


def per_device(sky_map, legendre, m_list, block_start, beam_ratio):
    cycle_rows = sky_map.shape[1]
    dev_count = lax.axis_size(("blk", "ma"))
    band_count = lax.axis_size("blk")
    owner_count = lax.axis_size("ma")
    m_values = m_list.reshape(-1)
    order_total = m_values.shape[0]
    own_count = m_list.shape[1]
    degree_width = legendre.shape[2]
    share_cols = degree_width // band_count
    first_cycle = lax.axis_index(("blk", "ma")) * cycle_rows
    parity = (first_cycle + jnp.arange(cycle_rows, dtype=jnp.int32)) % 2
    coeffs = cycle_fourier(sky_map, m_values, parity)
    factor_norm = 1.0 / math.sqrt(2.0 * cycle_rows * dev_count)
    owner_index = lax.axis_index("ma")
    band_index = lax.axis_index("blk")
    products = jnp.einsum("crm,rml->cml", coeffs, legendre, preferred_element_type=jnp.float32)
    column = jnp.arange(degree_width, dtype=jnp.int32)
    full_even = (column[None, :] + m_values[:, None]) % 2 == 0
    partial_sum = jnp.where(full_even[None], products[:2], products[2:]) * factor_norm
    arranged = partial_sum.reshape(2, owner_count, own_count, band_count, share_cols)
    arranged = jnp.transpose(arranged, (3, 1, 0, 2, 4)).reshape(
        band_count * owner_count * 2, own_count, share_cols
    )
    summed = lax.psum_scatter(arranged, ("blk", "ma"), scatter_dimension=0, tiled=True)
    own_blocks = lax.dynamic_slice_in_dim(block_start, owner_index * own_count, own_count, 0)
    ratio_table = beam_ratio.reshape(-1, LBLK)[own_blocks].reshape(own_count, degree_width)
    ratio_rows = lax.dynamic_slice_in_dim(ratio_table, band_index * share_cols, share_cols, 1)
    harmonics = summed * ratio_rows[None]
    spectrum = lax.psum(jnp.sum(harmonics * harmonics, axis=(0, 1)) / order_total, "ma")
    return (harmonics, spectrum)


def solution(mesh):
    placed = (P(None, ("blk", "ma"), None), P(("blk", "ma"), None, None), P(), P(), P())
    return jax.shard_map(
        per_device,
        mesh=mesh,
        in_specs=placed,
        out_specs=(P(None, "ma", "blk"), P("blk")),
        check_vma=False,
    )
```

profile of v0, /device:TPU:0, one launch (start us, length us, event | category | flops | bytes accessed | tf_op | source)
XLA Modules:
  0.0 358.5 jit_solution(4791145079997097095)
XLA Ops:
  7.2 0.0 reduce-scatter.2.cloned.1.call-start
  7.2 0.8 add.120
  8.0 0.8 mul.257
  8.8 0.6 fusion.28
  9.4 0.1 cosine_multiply_fusion
  9.5 174.3 %while.16 = (s32[]{:T(128)}, f32[16,64]{1,0:T(8,128)S(1)}, f32[16,64]{1,0:T(8,128)S(1)}, s32[8]{0:T(128)S(1)}, f32[16,65536]{1,0:T(8,128)}, /*index=5*/s32[4,16]...) while((s32[]{:T(128)}, f32[16,64]{1,0:T(8,128)S(1)}, ...), condition=%wide.wide.region_1.2_spmd.clone, body=%wide.wide.region_0.1_spmd.clone.sunk | while | flops 216018944 | bytes 1163966 | solution.py:36
  9.5 0.6 dynamic_slice.37
  10.8 10.3 %fusion.53 = f32[16,64]{1,0:T(8,128)S(1)} fusion(s32[64]{0:T(128)S(1)} %get-tuple-element.223, s32[8192]{0:T(1024)S(1)} %iota_add_fusion.3, f32[16,65536]{1,0:T(8,128)} %get-tuple-element.221, s32[]{:T(128)S(6)} %select_n.86, f32[16,64]{1,0:T(8,128)S(1)} %get-tuple-element.208, pred[]{:T(512)S(6)} %compare.13), kind=kOutput, calls=%fused_computation.14.clone.clone.1 | convolution fusion | flops 108005376 | bytes 565509 | tf_op jit(solution)/shard_map/while/body/eval_jaxpr/dot_general | solution.py:27
  21.0 10.2 %fusion.52 = f32[16,64]{1,0:T(8,128)S(1)} fusion(s32[64]{0:T(128)S(1)} %get-tuple-element.223, s32[8192]{0:T(1024)S(1)} %iota_add_fusion.3, f32[16,65536]{1,0:T(8,128)} %get-tuple-element.221, s32[]{:T(128)S(6)} %select_n.86, f32[16,64]{1,0:T(8,128)S(1)} %get-tuple-element.207, pred[]{:T(512)S(6)} %compare.13), kind=kOutput, calls=%fused_computation.13.clone.clone.1 | convolution fusion | flops 108005376 | bytes 565509 | tf_op jit(solution)/shard_map/while/body/eval_jaxpr/dot_general | solution.py:21
  31.3 0.6 dynamic_slice.37
  32.6 10.3 %fusion.53 = f32[16,64]{1,0:T(8,128)S(1)} fusion(s32[64]{0:T(128)S(1)} %get-tuple-element.223, s32[8192]{0:T(1024)S(1)} %iota_add_fusion.3, f32[16,65536]{1,0:T(8,128)} %get-tuple-element.221, s32[]{:T(128)S(6)} %select_n.86, f32[16,64]{1,0:T(8,128)S(1)} %get-tuple-element.208, pred[]{:T(512)S(6)} %compare.13), kind=kOutput, calls=%fused_computation.14.clone.clone.1 | convolution fusion | flops 108005376 | bytes 565509 | tf_op jit(solution)/shard_map/while/body/eval_jaxpr/dot_general | solution.py:27
  42.8 10.2 %fusion.52 = f32[16,64]{1,0:T(8,128)S(1)} fusion(s32[64]{0:T(128)S(1)} %get-tuple-element.223, s32[8192]{0:T(1024)S(1)} %iota_add_fusion.3, f32[16,65536]{1,0:T(8,128)} %get-tuple-element.221, s32[]{:T(128)S(6)} %select_n.86, f32[16,64]{1,0:T(8,128)S(1)} %get-tuple-element.207, pred[]{:T(512)S(6)} %compare.13), kind=kOutput, calls=%fused_computation.13.clone.clone.1 | convolution fusion | flops 108005376 | bytes 565509 | tf_op jit(solution)/shard_map/while/body/eval_jaxpr/dot_general | solution.py:21
  53.1 0.6 dynamic_slice.37
  54.3 10.3 %fusion.53 = f32[16,64]{1,0:T(8,128)S(1)} fusion(s32[64]{0:T(128)S(1)} %get-tuple-element.223, s32[8192]{0:T(1024)S(1)} %iota_add_fusion.3, f32[16,65536]{1,0:T(8,128)} %get-tuple-element.221, s32[]{:T(128)S(6)} %select_n.86, f32[16,64]{1,0:T(8,128)S(1)} %get-tuple-element.208, pred[]{:T(512)S(6)} %compare.13), kind=kOutput, calls=%fused_computation.14.clone.clone.1 | convolution fusion | flops 108005376 | bytes 565509 | tf_op jit(solution)/shard_map/while/body/eval_jaxpr/dot_general | solution.py:27
  64.6 10.2 %fusion.52 = f32[16,64]{1,0:T(8,128)S(1)} fusion(s32[64]{0:T(128)S(1)} %get-tuple-element.223, s32[8192]{0:T(1024)S(1)} %iota_add_fusion.3, f32[16,65536]{1,0:T(8,128)} %get-tuple-element.221, s32[]{:T(128)S(6)} %select_n.86, f32[16,64]{1,0:T(8,128)S(1)} %get-tuple-element.207, pred[]{:T(512)S(6)} %compare.13), kind=kOutput, calls=%fused_computation.13.clone.clone.1 | convolution fusion | flops 108005376 | bytes 565509 | tf_op jit(solution)/shard_map/while/body/eval_jaxpr/dot_general | solution.py:21
  74.8 0.6 dynamic_slice.37
  76.1 10.3 %fusion.53 = f32[16,64]{1,0:T(8,128)S(1)} fusion(s32[64]{0:T(128)S(1)} %get-tuple-element.223, s32[8192]{0:T(1024)S(1)} %iota_add_fusion.3, f32[16,65536]{1,0:T(8,128)} %get-tuple-element.221, s32[]{:T(128)S(6)} %select_n.86, f32[16,64]{1,0:T(8,128)S(1)} %get-tuple-element.208, pred[]{:T(512)S(6)} %compare.13), kind=kOutput, calls=%fused_computation.14.clone.clone.1 | convolution fusion | flops 108005376 | bytes 565509 | tf_op jit(solution)/shard_map/while/body/eval_jaxpr/dot_general | solution.py:27
  86.3 10.2 %fusion.52 = f32[16,64]{1,0:T(8,128)S(1)} fusion(s32[64]{0:T(128)S(1)} %get-tuple-element.223, s32[8192]{0:T(1024)S(1)} %iota_add_fusion.3, f32[16,65536]{1,0:T(8,128)} %get-tuple-element.221, s32[]{:T(128)S(6)} %select_n.86, f32[16,64]{1,0:T(8,128)S(1)} %get-tuple-element.207, pred[]{:T(512)S(6)} %compare.13), kind=kOutput, calls=%fused_computation.13.clone.clone.1 | convolution fusion | flops 108005376 | bytes 565509 | tf_op jit(solution)/shard_map/while/body/eval_jaxpr/dot_general | solution.py:21
  96.6 0.6 dynamic_slice.37
  97.9 10.3 %fusion.53 = f32[16,64]{1,0:T(8,128)S(1)} fusion(s32[64]{0:T(128)S(1)} %get-tuple-element.223, s32[8192]{0:T(1024)S(1)} %iota_add_fusion.3, f32[16,65536]{1,0:T(8,128)} %get-tuple-element.221, s32[]{:T(128)S(6)} %select_n.86, f32[16,64]{1,0:T(8,128)S(1)} %get-tuple-element.208, pred[]{:T(512)S(6)} %compare.13), kind=kOutput, calls=%fused_computation.14.clone.clone.1 | convolution fusion | flops 108005376 | bytes 565509 | tf_op jit(solution)/shard_map/while/body/eval_jaxpr/dot_general | solution.py:27
  108.1 10.2 %fusion.52 = f32[16,64]{1,0:T(8,128)S(1)} fusion(s32[64]{0:T(128)S(1)} %get-tuple-element.223, s32[8192]{0:T(1024)S(1)} %iota_add_fusion.3, f32[16,65536]{1,0:T(8,128)} %get-tuple-element.221, s32[]{:T(128)S(6)} %select_n.86, f32[16,64]{1,0:T(8,128)S(1)} %get-tuple-element.207, pred[]{:T(512)S(6)} %compare.13), kind=kOutput, calls=%fused_computation.13.clone.clone.1 | convolution fusion | flops 108005376 | bytes 565509 | tf_op jit(solution)/shard_map/while/body/eval_jaxpr/dot_general | solution.py:21
  118.4 0.6 dynamic_slice.37
  119.6 10.3 %fusion.53 = f32[16,64]{1,0:T(8,128)S(1)} fusion(s32[64]{0:T(128)S(1)} %get-tuple-element.223, s32[8192]{0:T(1024)S(1)} %iota_add_fusion.3, f32[16,65536]{1,0:T(8,128)} %get-tuple-element.221, s32[]{:T(128)S(6)} %select_n.86, f32[16,64]{1,0:T(8,128)S(1)} %get-tuple-element.208, pred[]{:T(512)S(6)} %compare.13), kind=kOutput, calls=%fused_computation.14.clone.clone.1 | convolution fusion | flops 108005376 | bytes 565509 | tf_op jit(solution)/shard_map/while/body/eval_jaxpr/dot_general | solution.py:27
  129.9 10.2 %fusion.52 = f32[16,64]{1,0:T(8,128)S(1)} fusion(s32[64]{0:T(128)S(1)} %get-tuple-element.223, s32[8192]{0:T(1024)S(1)} %iota_add_fusion.3, f32[16,65536]{1,0:T(8,128)} %get-tuple-element.221, s32[]{:T(128)S(6)} %select_n.86, f32[16,64]{1,0:T(8,128)S(1)} %get-tuple-element.207, pred[]{:T(512)S(6)} %compare.13), kind=kOutput, calls=%fused_computation.13.clone.clone.1 | convolution fusion | flops 108005376 | bytes 565509 | tf_op jit(solution)/shard_map/while/body/eval_jaxpr/dot_general | solution.py:21
  140.1 0.6 dynamic_slice.37
  141.4 10.3 %fusion.53 = f32[16,64]{1,0:T(8,128)S(1)} fusion(s32[64]{0:T(128)S(1)} %get-tuple-element.223, s32[8192]{0:T(1024)S(1)} %iota_add_fusion.3, f32[16,65536]{1,0:T(8,128)} %get-tuple-element.221, s32[]{:T(128)S(6)} %select_n.86, f32[16,64]{1,0:T(8,128)S(1)} %get-tuple-element.208, pred[]{:T(512)S(6)} %compare.13), kind=kOutput, calls=%fused_computation.14.clone.clone.1 | convolution fusion | flops 108005376 | bytes 565509 | tf_op jit(solution)/shard_map/while/body/eval_jaxpr/dot_general | solution.py:27
  151.7 10.2 %fusion.52 = f32[16,64]{1,0:T(8,128)S(1)} fusion(s32[64]{0:T(128)S(1)} %get-tuple-element.223, s32[8192]{0:T(1024)S(1)} %iota_add_fusion.3, f32[16,65536]{1,0:T(8,128)} %get-tuple-element.221, s32[]{:T(128)S(6)} %select_n.86, f32[16,64]{1,0:T(8,128)S(1)} %get-tuple-element.207, pred[]{:T(512)S(6)} %compare.13), kind=kOutput, calls=%fused_computation.13.clone.clone.1 | convolution fusion | flops 108005376 | bytes 565509 | tf_op jit(solution)/shard_map/while/body/eval_jaxpr/dot_general | solution.py:21
  161.9 0.6 dynamic_slice.37
  163.2 10.3 %fusion.53 = f32[16,64]{1,0:T(8,128)S(1)} fusion(s32[64]{0:T(128)S(1)} %get-tuple-element.223, s32[8192]{0:T(1024)S(1)} %iota_add_fusion.3, f32[16,65536]{1,0:T(8,128)} %get-tuple-element.221, s32[]{:T(128)S(6)} %select_n.86, f32[16,64]{1,0:T(8,128)S(1)} %get-tuple-element.208, pred[]{:T(512)S(6)} %compare.13), kind=kOutput, calls=%fused_computation.14.clone.clone.1 | convolution fusion | flops 108005376 | bytes 565509 | tf_op jit(solution)/shard_map/while/body/eval_jaxpr/dot_general | solution.py:27
  173.4 10.2 %fusion.52 = f32[16,64]{1,0:T(8,128)S(1)} fusion(s32[64]{0:T(128)S(1)} %get-tuple-element.223, s32[8192]{0:T(1024)S(1)} %iota_add_fusion.3, f32[16,65536]{1,0:T(8,128)} %get-tuple-element.221, s32[]{:T(128)S(6)} %select_n.86, f32[16,64]{1,0:T(8,128)S(1)} %get-tuple-element.207, pred[]{:T(512)S(6)} %compare.13), kind=kOutput, calls=%fused_computation.13.clone.clone.1 | convolution fusion | flops 108005376 | bytes 565509 | tf_op jit(solution)/shard_map/while/body/eval_jaxpr/dot_general | solution.py:21
  183.9 0.1 copy.20
  184.0 7.1 %convolution_bitcast_fusion = f32[4,64,4096]{2,0,1:T(4,128)S(1)} fusion(bf16[4,8,64]{1,0,2:T(4,128)(2,1)S(1)} %copy.20, bf16[8,64,4096]{2,1,0:T(8,128)(2,1)} %param.8), kind=kOutput, calls=%fused_computation.26 | convolution fusion | flops 16777216 | bytes 8392704 | tf_op jit(solution)/shard_map/crm,rml->cml/dot_general | solution.py:74
  191.2 2.1 fusion.26
  193.2 2.8 reshape.148
  196.1 4.2 %copy.22 = f32[8,4,2,16,512]{4,3,2,1,0:T(8,128)} copy(f32[8,4,2,16,512]{4,0,2,3,1:T(8,128)} %bitcast.27) | data formatting | bytes 4194304 | tf_op jit(solution)/shard_map/transpose | solution.py:79
  200.2 0.0 copy-start
  200.2 0.0 reduce-scatter.2.cloned.1.call-update
  200.2 0.7 compare_select_fusion
  201.0 0.1 reshape.154
  201.0 0.1 copy-done
  201.1 0.1 reshape.150
  201.2 2.8 gather_fusion
  204.1 0.2 reshape.151
  204.3 137.0 %reduce-scatter.2.cloned.1.call-done = f32[2,16,512]{2,1,0:T(8,128)} async-done(((f32[64,16,512]{2,1,0:T(8,128)}), f32[2,16,512]{2,1,0:T(8,128)}) %reduce-scatter.2.cloned.1.call-update) | async-done | bytes 65552 | tf_op jit(solution)/shard_map/reduce_scatter | solution.py:82
  341.3 1.5 multiply_reduce_fusion
  342.8 8.9 %psum.7 = f32[512]{0:T(512)} all-reduce(f32[512]{0:T(512)S(1)} %broadcast_multiply_fusion.1), channel_id=1, replica_groups=mesh['blk'=8,'ma'=4] {'ma'}, use_global_device_ids=true, to_apply=%region_4.5 | all-reduce | flops 512 | bytes 4096 | tf_op jit(solution)/shard_map/psum | solution.py:87
  (18 shorter events, 0.1 us)
Async XLA Ops:
  7.2 334.1 %reduce-scatter.2.cloned.1.call-start = ((), (), s32[]{:S(2)}) async-start(), calls=%async_computation.1 | async-start | bytes 2162688 | tf_op jit(solution)/shard_map/reduce_scatter | solution.py:82
  200.2 0.9 copy-start
Sparse Core Ops, SparseCore 0:
  200.4 140.9 reduce-scatter.1
where the time goes:
time: 360 us; the launch traced here: 359 us
  matrix products  171 us (48%)
  waiting for transfers between devices  137 us (38%)
  local copies, waits for them, and re-layouts  16.6 us (5%)
  between operations  14.1 us (4%)
  blocking collectives  8.91 us (2%)
  loops' own time  5.7 us (2%)
  other arithmetic  5.11 us (1%)
    reduce_scatter x1, waiting for transfers between devices, per_device(): lax.psum_scatter(arranged, ('blk', 'ma'), scatter_dimension=0, tiled=True)  137 us
    dot_general x8, matrix products, add_block(): jnp.dot(segment, jnp.sin(angles), precision=lax.Precision.HIGHEST, prefer...  82 us
    dot_general x8, matrix products, add_block(): jnp.dot(segment, jnp.cos(angles), precision=lax.Precision.HIGHEST, prefer...  81.9 us
    psum x1, blocking collectives, per_device(): lax.psum(jnp.sum(harmonics * harmonics, axis=(0, 1)) / order_total, 'ma')  8.91 us
  transfers between devices with their start and end apart: 1, of which 1 were waited for; matrix products, arithmetic and copies ran while one was open for 1% of the time, Pallas kernels for 0%

commit v1 on v0

v1 whole, which is shorter than its diff:
```python
import functools
import math

import jax
import jax.numpy as jnp
from jax import lax
from jax.experimental import pallas as pl
from jax.experimental.pallas import tpu as pltpu
from jax.sharding import PartitionSpec as P

LBLK = 64
LANES = 128
MESH = pl.DeviceIdType.MESH


def cos_sin(steps, per_turn):
    quarter = per_turn // 4
    shift = quarter.bit_length() - 1
    quadrant = lax.shift_right_arithmetic(steps + quarter // 2, shift)
    y = (steps - quadrant * quarter).astype(jnp.float32) * (2.0 * math.pi / per_turn)
    z = y * y
    s = y * (1.0 + z * (-1.0 / 6 + z * (1.0 / 120 + z * (-1.0 / 5040 + z * (1.0 / 362880)))))
    c = 1.0 + z * (-0.5 + z * (1.0 / 24 + z * (-1.0 / 720 + z * (1.0 / 40320))))
    swap = (quadrant & 1) == 1
    cos = jnp.where(swap, s, c)
    sin = jnp.where(swap, c, s)
    cos = jnp.where(((quadrant + 1) & 2) == 2, -cos, cos)
    sin = jnp.where((quadrant & 2) == 2, -sin, sin)
    return cos, sin


def kernel(
    dims,
    sky_hbm,
    leg_hbm,
    m_ref,
    block_ref,
    beam_ref,
    harm_ref,
    spec_ref,
    sky,
    leg,
    fine,
    coarse,
    lhs,
    psend,
    own,
    precv,
    xsend,
    xrecv,
    plane_sum,
    zsend,
    zrecv,
    ratio,
    beam2,
    power,
    precv_power,
    sky_sem,
    leg_sem,
    psem,
    xsem,
    zsem,
    ssem,
):
    blk_n, ma_n, cycles, orders, own_n, degrees, npix, pieces = dims
    planes = blk_n // 2
    share = degrees // blk_n
    chunks = share // LANES
    period = 2 * orders
    q_all = npix // period
    q_fine = 16
    q_coarse = q_all // q_fine
    blk = lax.axis_index("blk")
    z = lax.axis_index("ma")
    core = blk % 2
    plane = blk // 2

    def flip(value, d):
        out, bit = 0, 1
        while bit <= d or bit == 1:
            digit = (value // bit) % 2
            out = out + bit * ((1 - digit) if d & bit else digit)
            bit *= 2
        return out + (value // bit) * bit

    sibling = (plane * 2 + 1 - core, z)
    plane_to = {d: flip(plane, d) for d in range(1, planes)}
    z_to = {d: flip(z, d) for d in range(1, ma_n)}

    width = npix // pieces
    sky_copies = [
        pltpu.make_async_copy(
            sky_hbm.at[:, :, pl.ds(i * width, width)],
            sky.at[:, :, pl.ds(i * width, width)],
            sky_sem.at[i],
        )
        for i in range(pieces)
    ]
    leg_copy = pltpu.make_async_copy(leg_hbm, leg, leg_sem)
    for copy in sky_copies:
        copy.start()
    leg_copy.start()

    barrier = pltpu.get_barrier_semaphore()
    partners = [sibling]
    partners += [(plane_to[d] * 2 + core, z) for d in range(1, planes)]
    partners += [(blk, z_to[d]) for d in range(1, ma_n)]
    for partner in partners:
        pl.semaphore_signal(barrier, inc=1, device_id=partner, device_id_type=MESH)

    m0 = m_ref[0, 0]
    lane = lax.broadcasted_iota(jnp.int32, (8, LANES), 1)
    m_vec = jnp.zeros((8, LANES), jnp.int32)
    for k in range(orders):
        m_vec = jnp.where(lane % orders == k, m_ref[k // own_n, k % own_n], m_vec)

    def fill(ref, count, step):
        index = lax.broadcasted_iota(jnp.int32, (count, 8, period), 0)
        c, s = cos_sin((index * (step * m0 % q_all)) % q_all, q_all)
        ref[0] = c
        ref[1] = s

    fill(fine, q_fine, 1)
    fill(coarse, q_coarse, q_fine)

    r_index = lax.broadcasted_iota(jnp.int32, (period, LANES), 0)
    tc, ts = cos_sin((r_index * m_vec[0:1]) % npix, npix)
    table = jnp.concatenate([tc, ts], axis=1)
    g_index = lax.broadcasted_iota(jnp.int32, (cycles, LANES), 0)
    first = (blk * ma_n + z) * cycles
    twist_c, twist_s = cos_sin(m_vec[0:1] * ((g_index + first) % 2), 2 * npix)

    zero = jnp.zeros((cycles, period), jnp.float32)

    def outer(i, acc):
        nc, ns, sc, ss = zero, zero, zero, zero
        for f in range(q_fine):
            at = pl.multiple_of((i * q_fine + f) * period, period)
            c, s = fine[0, f], fine[1, f]
            north = sky[0, :, pl.ds(at, period)]
            south = sky[1, :, pl.ds(at, period)]
            nc, ns = nc + north * c, ns + north * s
            sc, ss = sc + south * c, ss + south * s
        c, s = coarse[0, i], coarse[1, i]
        return (
            acc[0] + (nc * c - ns * s),
            acc[1] + (nc * s + ns * c),
            acc[2] + (sc * c - ss * s),
            acc[3] + (sc * s + ss * c),
        )

    acc = (zero, zero, zero, zero)
    per_piece = q_coarse // pieces
    for i in range(pieces):
        sky_copies[i].wait()
        acc = lax.fori_loop(i * per_piece, (i + 1) * per_piece, outer, acc)
    north_c, north_s, south_c, south_s = acc
    rows = jnp.concatenate(
        [north_c + south_c, north_c - south_c, north_s + south_s, north_s - south_s], axis=0
    )
    prod = jnp.dot(
        rows, table, precision=lax.Precision.HIGHEST, preferred_element_type=jnp.float32
    )
    scale = 1.0 / math.sqrt(npix)
    coeffs = []
    for h in range(2):
        by_c = prod[h * cycles : (h + 1) * cycles]
        by_s = prod[(2 + h) * cycles : (3 + h) * cycles]
        re = (by_c[:, :LANES] - by_s[:, LANES:]) * scale
        im = (by_c[:, LANES:] + by_s[:, :LANES]) * -scale
        coeffs.append(re * twist_c + im * twist_s)
        coeffs.append(im * twist_c - re * twist_s)

    dup = LANES // orders
    row = lax.broadcasted_iota(jnp.int32, (orders, LANES), 0)
    col = lax.broadcasted_iota(jnp.int32, (orders, LANES), 1)
    diagonal = row == col % orders
    for c in range(4):
        for p in range(cycles // dup):
            line = coeffs[c][p * dup : p * dup + 1]
            for e in range(1, dup):
                line = jnp.where(lane[0:1] >= e * orders, coeffs[c][p * dup + e : p * dup + e + 1], line)
            lhs[c * orders : (c + 1) * orders, p * LANES : (p + 1) * LANES] = jnp.where(
                diagonal, line, 0.0
            ).astype(jnp.bfloat16)

    even_lane = (lax.broadcasted_iota(jnp.int32, (2 * orders, 2 * LANES), 1) + m0) % 2 == 0
    leg_copy.wait()

    def contract(side, t, p):
        parts = []
        for e in range(2):
            at = pl.multiple_of((2 * (p + e) + side) * share + t * LANES, LANES)
            parts.append(leg[:, :, pl.ds(at, LANES)].reshape(cycles * orders, LANES))
        res = jnp.dot(
            lhs[...], jnp.concatenate(parts, axis=1), preferred_element_type=jnp.float32
        )
        return jnp.where(even_lane, res[: 2 * orders], res[2 * orders :])

    pcopies, xcopies, zcopies = {}, {}, {}

    def multiply(t):
        for p in range(0, planes, 2):
            res = contract(1 - core, t, p).astype(jnp.bfloat16)
            psend[t, p] = res[:, :LANES]
            psend[t, p + 1] = res[:, LANES:]
        if t == 0:
            pl.semaphore_wait(barrier, len(partners))
        pcopies[t] = pltpu.make_async_remote_copy(
            src_ref=psend.at[t],
            dst_ref=precv.at[t],
            send_sem=psem.at[0, t],
            recv_sem=psem.at[1, t],
            device_id=sibling,
            device_id_type=MESH,
        )
        pcopies[t].start()
        for p in range(0, planes, 2):
            res = contract(core, t, p)
            own[t, p] = res[:, :LANES]
            own[t, p + 1] = res[:, LANES:]

    def to_plane(t):
        pcopies[t].wait_recv()
        for d in range(planes - 1, 0, -1):
            other = plane_to[d]
            xsend[t, d - 1] = (own[t, other] + precv[t, other].astype(jnp.float32)).astype(
                jnp.bfloat16
            )
            copy = pltpu.make_async_remote_copy(
                src_ref=xsend.at[t, d - 1],
                dst_ref=xrecv.at[t, d - 1],
                send_sem=xsem.at[0, t, d - 1],
                recv_sem=xsem.at[1, t, d - 1],
                device_id=(other * 2 + core, z),
                device_id_type=MESH,
            )
            copy.start()
            xcopies[t, d] = copy

    def to_z(t):
        total = own[t, plane] + precv[t, plane].astype(jnp.float32)
        for d in range(1, planes):
            xcopies[t, d].wait_recv()
            total = total + xrecv[t, d - 1].astype(jnp.float32)
        plane_sum[t] = total.reshape(2, ma_n, own_n, LANES)
        for d in range(ma_n - 1, 0, -1):
            zsend[t, d - 1] = plane_sum[t, :, z_to[d]].astype(jnp.bfloat16)
            copy = pltpu.make_async_remote_copy(
                src_ref=zsend.at[t, d - 1],
                dst_ref=zrecv.at[t, d - 1],
                send_sem=zsem.at[0, t, d - 1],
                recv_sem=zsem.at[1, t, d - 1],
                device_id=(blk, z_to[d]),
                device_id_type=MESH,
            )
            copy.start()
            zcopies[t, d] = copy

    def beam_rows():
        rows_n = beam_ref.shape[0]
        beam2[:rows_n] = beam_ref[...]
        beam2[rows_n:] = pltpu.roll(beam_ref[...], LBLK, 1)
        low = lax.broadcasted_iota(jnp.int32, (1, LANES), 1) < LBLK

        def one(i, carry):
            for t in range(chunks):
                column = blk * (share // LBLK) + 2 * t
                b0 = block_ref[z * own_n + i, column]
                b1 = block_ref[z * own_n + i, column + 1]
                left = beam2[pl.ds((b0 % 2) * rows_n + b0 // 2, 1), :]
                right = beam2[pl.ds((1 - b1 % 2) * rows_n + b1 // 2, 1), :]
                ratio[t, pl.ds(i, 1), :] = jnp.where(low, left, right)
            return carry

        lax.fori_loop(0, own_n, one, 0)

    norm = 1.0 / math.sqrt(2.0 * cycles * blk_n * ma_n)

    def finish(t):
        total = plane_sum[t, :, z]
        for d in range(1, ma_n):
            zcopies[t, d].wait_recv()
            total = total + zrecv[t, d - 1].astype(jnp.float32)
        harm = total * norm * ratio[t][None]
        harm_ref[:, :, t * LANES : (t + 1) * LANES] = harm
        squares = jnp.sum(harm * harm, axis=(0, 1)) * (1.0 / orders)
        power[t : t + 1] = squares.reshape(1, LANES)

    for step in range(chunks + 3):
        if step < chunks:
            multiply(step)
        if 1 <= step <= chunks:
            to_plane(step - 1)
        if step == 2:
            beam_rows()
        if 2 <= step <= chunks + 1:
            to_z(step - 2)
        if 3 <= step:
            finish(step - 3)

    scopies = []
    for d in range(1, ma_n):
        copy = pltpu.make_async_remote_copy(
            src_ref=power,
            dst_ref=precv_power.at[d - 1],
            send_sem=ssem.at[0, d - 1],
            recv_sem=ssem.at[1, d - 1],
            device_id=(blk, z_to[d]),
            device_id_type=MESH,
        )
        copy.start()
        scopies.append(copy)
    for t in range(chunks):
        pcopies[t].wait_send()
        for d in range(1, planes):
            xcopies[t, d].wait_send()
        for d in range(1, ma_n):
            zcopies[t, d].wait_send()
    spectrum = power[...]
    for d in range(1, ma_n):
        scopies[d - 1].wait()
        spectrum = spectrum + precv_power[d - 1]
    for t in range(chunks):
        spec_ref[:, t * LANES : (t + 1) * LANES] = spectrum[t : t + 1]


def per_device(blk_n, ma_n, sky_map, legendre, m_list, block_start, beam_ratio):
    npix = sky_map.shape[2]
    cycles, orders, degrees = legendre.shape
    own_n = m_list.shape[1]
    share = degrees // blk_n
    chunks = share // LANES
    planes = blk_n // 2
    period = 2 * orders
    q_all = npix // period
    pieces = 4
    dims = (blk_n, ma_n, cycles, orders, own_n, degrees, npix, pieces)
    beam = beam_ratio.reshape(-1, LANES)
    f32, bf16 = jnp.float32, jnp.bfloat16
    dma = pltpu.SemaphoreType.DMA
    vmem = pl.BlockSpec(memory_space=pltpu.VMEM)
    smem = pl.BlockSpec(memory_space=pltpu.SMEM)
    anywhere = pl.BlockSpec(memory_space=pl.ANY)
    harm, spec = pl.pallas_call(
        functools.partial(kernel, dims),
        out_shape=(
            jax.ShapeDtypeStruct((2, own_n, share), f32),
            jax.ShapeDtypeStruct((1, share), f32),
        ),
        in_specs=[anywhere, anywhere, smem, smem, vmem],
        out_specs=(vmem, vmem),
        scratch_shapes=[
            pltpu.VMEM(sky_map.shape, f32),
            pltpu.VMEM(legendre.shape, bf16),
            pltpu.VMEM((2, 16, 8, period), f32),
            pltpu.VMEM((2, q_all // 16, 8, period), f32),
            pltpu.VMEM((4 * orders, cycles * orders), bf16),
            pltpu.VMEM((chunks, planes, 2 * orders, LANES), bf16),
            pltpu.VMEM((chunks, planes, 2 * orders, LANES), f32),
            pltpu.VMEM((chunks, planes, 2 * orders, LANES), bf16),
            pltpu.VMEM((chunks, planes - 1, 2 * orders, LANES), bf16),
            pltpu.VMEM((chunks, planes - 1, 2 * orders, LANES), bf16),
            pltpu.VMEM((chunks, 2, ma_n, own_n, LANES), f32),
            pltpu.VMEM((chunks, ma_n - 1, 2, own_n, LANES), bf16),
            pltpu.VMEM((chunks, ma_n - 1, 2, own_n, LANES), bf16),
            pltpu.VMEM((chunks, own_n, LANES), f32),
            pltpu.VMEM((2 * beam.shape[0], LANES), f32),
            pltpu.VMEM((chunks, LANES), f32),
            pltpu.VMEM((ma_n - 1, chunks, LANES), f32),
            dma((pieces,)),
            dma,
            dma((2, chunks)),
            dma((2, chunks, planes - 1)),
            dma((2, chunks, ma_n - 1)),
            dma((2, ma_n - 1)),
        ],
        compiler_params=pltpu.CompilerParams(
            collective_id=0, has_side_effects=True, vmem_limit_bytes=56 * 1024 * 1024
        ),
    )(sky_map, legendre, m_list, block_start, beam)
    return harm, spec.reshape(share)


def solution(mesh):
    placed = (P(None, ("blk", "ma"), None), P(("blk", "ma"), None, None), P(), P(), P())
    return jax.shard_map(
        functools.partial(per_device, mesh.shape["blk"], mesh.shape["ma"]),
        mesh=mesh,
        in_specs=placed,
        out_specs=(P(None, "ma", "blk"), P("blk")),
        check_vma=False,
    )
```

time: 360 us -> 33.1 us (0.09)
  matrix products: 171 us -> 0 us
  waiting for transfers between devices: 137 us -> 0 us
  Pallas kernels: 0 us -> 29.5 us
  local copies, waits for them, and re-layouts: 16.6 us -> 2.72 us
  between operations: 14.1 us -> 0.64 us
  blocking collectives: 8.91 us -> 0 us
  loops' own time: 5.7 us -> 0 us
  other arithmetic: 5.11 us -> 0 us
    dot_general x17 -> x0, matrix products: 171 us -> none  [the longest x8 82 us: add_block(): jnp.dot(segment, jnp.sin(angles), precision=lax.Precision.HIGHEST, prefer...]
    reduce_scatter x1 -> x0, waiting for transfers between devices: 137 us -> none  [per_device(): lax.psum_scatter(arranged, ('blk', 'ma'), scatter_dimension=0, tiled=True)]
    pallas_call x0 -> x1, Pallas kernels: none -> 29.5 us  [per_device(): pl.pallas_call(functools.partial(kernel, dims), out_shape=(jax.ShapeDtype...]
    psum x1 -> x0, blocking collectives: 8.91 us -> none  [per_device(): lax.psum(jnp.sum(harmonics * harmonics, axis=(0, 1)) / order_total, 'ma')]
    another operation x1 -> x0, loops' own time: 5.7 us -> none  [cycle_fourier(): lax.scan(add_block, (empty_acc, empty_acc), jnp.arange(pixel_count // blo...]
    dynamic_slice x9 -> x0, local copies, waits for them, and re-layouts: 4.7 us -> none  [the longest x8 4.69 us: cycle_fourier(): lax.scan(add_block, (empty_acc, empty_acc), jnp.arange(pixel_count // blo...]
    transpose x1 -> x0, local copies, waits for them, and re-layouts: 4.15 us -> none  [per_device(): jnp.transpose(arranged, (3, 1, 0, 2, 4))]
  transfers between devices with their start and end apart: 1 -> 0, of which waited for: 1 -> 0; matrix products, arithmetic and copies ran while one was open for 1% -> 0% of each run, Pallas kernels for 0% -> 0%
where the time goes in v1:
time: 33.1 us; the launch traced here: 32.9 us
  Pallas kernels  29.5 us (89%)
  local copies, waits for them, and re-layouts  2.72 us (8%)
  between operations  0.64 us (2%)
    pallas_call x1, Pallas kernels, per_device(): pl.pallas_call(functools.partial(kernel, dims), out_shape=(jax.ShapeDtype...  29.5 us
    unnamed x2, local copies, waits for them, and re-layouts  2.72 us

profile of v1, /device:TPU:0, one launch (start us, length us, event | category | flops | bytes accessed | tf_op | source)
XLA Modules:
  0.0 32.9 jit_solution(18266188166073494125)
XLA Ops:
  0.6 29.5 %shard_map.68 = (f32[2,16,512]{2,1,0:T(8,128)}, f32[1,512]{1,0:T(1,128)}) custom-call(f32[2,8,65536]{2,1,0:T(8,128)} %sky_hbm.1, bf16[8,64,4096]{2,1,0:T(8,128)(2,1)} %leg_hbm.1, s32[4,16]{1,0:T(4,128)} %m_ref.1, s32[64,64]{1,0:T(8,128)} %block_ref.1, f32[256,128]{1,0:T(8,128)} %bitcast.2), custom_call_target="tpu_custom_call" | custom-call | tf_op jit(solution)/shard_map/pallas_call | solution.py:345
  30.1 1.5 %copy.9 = f32[2,16,512]{2,1,0:T(8,128)} copy(f32[2,16,512]{2,1,0:T(8,128)} %get-tuple-element.8) | data formatting | bytes 131072
  31.6 1.2 %copy.10 = f32[512]{0:T(512)} copy(f32[512]{0:T(512)} %bitcast.3) | data formatting | bytes 4096

commit v2 on v1

--- a/solution.py
+++ b/solution.py
@@ -9,6 +9,7 @@
 from jax.sharding import PartitionSpec as P
 
 LBLK = 64
+CHUNKS = 2
 LANES = 128
 MESH = pl.DeviceIdType.MESH
 
@@ -33,11 +34,14 @@
     dims,
     sky_hbm,
     leg_hbm,
+    m_hbm,
+    block_hbm,
+    beam_hbm,
+    harm_ref,
+    spec_ref,
     m_ref,
     block_ref,
     beam_ref,
-    harm_ref,
-    spec_ref,
     sky,
     leg,
     fine,
@@ -55,6 +59,7 @@
     beam2,
     power,
     precv_power,
+    small_sem,
     sky_sem,
     leg_sem,
     psem,
@@ -62,10 +67,10 @@
     zsem,
     ssem,
 ):
-    blk_n, ma_n, cycles, orders, own_n, degrees, npix, pieces = dims
+    blk_n, ma_n, cycles, orders, own_n, degrees, npix, pieces, chunks = dims
     planes = blk_n // 2
     share = degrees // blk_n
-    chunks = share // LANES
+    wide = share // chunks
     period = 2 * orders
     q_all = npix // period
     q_fine = 16
@@ -97,6 +102,12 @@
         for i in range(pieces)
     ]
     leg_copy = pltpu.make_async_copy(leg_hbm, leg, leg_sem)
+    m_copy = pltpu.make_async_copy(m_hbm, m_ref, small_sem.at[0])
+    block_copy = pltpu.make_async_copy(block_hbm, block_ref, small_sem.at[1])
+    beam_copy = pltpu.make_async_copy(beam_hbm, beam_ref, small_sem.at[2])
+    m_copy.start()
+    block_copy.start()
+    beam_copy.start()
     for copy in sky_copies:
         copy.start()
     leg_copy.start()
@@ -108,6 +119,7 @@
     for partner in partners:
         pl.semaphore_signal(barrier, inc=1, device_id=partner, device_id_type=MESH)
 
+    m_copy.wait()
     m0 = m_ref[0, 0]
     lane = lax.broadcasted_iota(jnp.int32, (8, LANES), 1)
     m_vec = jnp.zeros((8, LANES), jnp.int32)
@@ -129,6 +141,28 @@
     g_index = lax.broadcasted_iota(jnp.int32, (cycles, LANES), 0)
     first = (blk * ma_n + z) * cycles
     twist_c, twist_s = cos_sin(m_vec[0:1] * ((g_index + first) % 2), 2 * npix)
+
+    def beam_rows():
+        rows_n = beam_ref.shape[0]
+        beam2[:rows_n] = beam_ref[...]
+        beam2[rows_n:] = pltpu.roll(beam_ref[...], LBLK, 1)
+        low = lax.broadcasted_iota(jnp.int32, (1, LANES), 1) < LBLK
+
+        def one(i, carry):
+            for t in range(share // LANES):
+                column = blk * (share // LBLK) + 2 * t
+                b0 = block_ref[z * own_n + i, column]
+                b1 = block_ref[z * own_n + i, column + 1]
+                left = beam2[pl.ds((b0 % 2) * rows_n + b0 // 2, 1), :]
+                right = beam2[pl.ds((1 - b1 % 2) * rows_n + b1 // 2, 1), :]
+                ratio[t, pl.ds(i, 1), :] = jnp.where(low, left, right)
+            return carry
+
+        lax.fori_loop(0, own_n, one, 0)
+
+    block_copy.wait()
+    beam_copy.wait()
+    beam_rows()
 
     zero = jnp.zeros((cycles, period), jnp.float32)
 
@@ -184,26 +218,26 @@
                 diagonal, line, 0.0
             ).astype(jnp.bfloat16)
 
-    even_lane = (lax.broadcasted_iota(jnp.int32, (2 * orders, 2 * LANES), 1) + m0) % 2 == 0
+    group = max(1, 2 * LANES // wide)
+    even_lane = (lax.broadcasted_iota(jnp.int32, (2 * orders, group * wide), 1) + m0) % 2 == 0
     leg_copy.wait()
 
     def contract(side, t, p):
         parts = []
-        for e in range(2):
-            at = pl.multiple_of((2 * (p + e) + side) * share + t * LANES, LANES)
-            parts.append(leg[:, :, pl.ds(at, LANES)].reshape(cycles * orders, LANES))
-        res = jnp.dot(
-            lhs[...], jnp.concatenate(parts, axis=1), preferred_element_type=jnp.float32
-        )
+        for e in range(group):
+            at = pl.multiple_of((2 * (p + e) + side) * share + t * wide, LANES)
+            parts.append(leg[:, :, pl.ds(at, wide)].reshape(cycles * orders, wide))
+        right = parts[0] if group == 1 else jnp.concatenate(parts, axis=1)
+        res = jnp.dot(lhs[...], right, preferred_element_type=jnp.float32)
         return jnp.where(even_lane, res[: 2 * orders], res[2 * orders :])
 
     pcopies, xcopies, zcopies = {}, {}, {}
 
     def multiply(t):
-        for p in range(0, planes, 2):
+        for p in range(0, planes, group):
             res = contract(1 - core, t, p).astype(jnp.bfloat16)
-            psend[t, p] = res[:, :LANES]
-            psend[t, p + 1] = res[:, LANES:]
+            for e in range(group):
+                psend[t, p + e] = res[:, e * wide : (e + 1) * wide]
         if t == 0:
             pl.semaphore_wait(barrier, len(partners))
         pcopies[t] = pltpu.make_async_remote_copy(
@@ -215,10 +249,10 @@
             device_id_type=MESH,
         )
         pcopies[t].start()
-        for p in range(0, planes, 2):
+        for p in range(0, planes, group):
             res = contract(core, t, p)
-            own[t, p] = res[:, :LANES]
-            own[t, p + 1] = res[:, LANES:]
+            for e in range(group):
+                own[t, p + e] = res[:, e * wide : (e + 1) * wide]
 
     def to_plane(t):
         pcopies[t].wait_recv()
@@ -243,7 +277,7 @@
         for d in range(1, planes):
             xcopies[t, d].wait_recv()
             total = total + xrecv[t, d - 1].astype(jnp.float32)
-        plane_sum[t] = total.reshape(2, ma_n, own_n, LANES)
+        plane_sum[t] = total.reshape(2, ma_n, own_n, wide)
         for d in range(ma_n - 1, 0, -1):
             zsend[t, d - 1] = plane_sum[t, :, z_to[d]].astype(jnp.bfloat16)
             copy = pltpu.make_async_remote_copy(
@@ -257,24 +291,6 @@
             copy.start()
             zcopies[t, d] = copy
 
-    def beam_rows():
-        rows_n = beam_ref.shape[0]
-        beam2[:rows_n] = beam_ref[...]
-        beam2[rows_n:] = pltpu.roll(beam_ref[...], LBLK, 1)
-        low = lax.broadcasted_iota(jnp.int32, (1, LANES), 1) < LBLK
-
-        def one(i, carry):
-            for t in range(chunks):
-                column = blk * (share // LBLK) + 2 * t
-                b0 = block_ref[z * own_n + i, column]
-                b1 = block_ref[z * own_n + i, column + 1]
-                left = beam2[pl.ds((b0 % 2) * rows_n + b0 // 2, 1), :]
-                right = beam2[pl.ds((1 - b1 % 2) * rows_n + b1 // 2, 1), :]
-                ratio[t, pl.ds(i, 1), :] = jnp.where(low, left, right)
-            return carry
-
-        lax.fori_loop(0, own_n, one, 0)
-
     norm = 1.0 / math.sqrt(2.0 * cycles * blk_n * ma_n)
 
     def finish(t):
@@ -282,18 +298,18 @@
         for d in range(1, ma_n):
             zcopies[t, d].wait_recv()
             total = total + zrecv[t, d - 1].astype(jnp.float32)
-        harm = total * norm * ratio[t][None]
-        harm_ref[:, :, t * LANES : (t + 1) * LANES] = harm
+        tiles = wide // LANES
+        beam_rows_t = jnp.concatenate([ratio[t * tiles + i] for i in range(tiles)], axis=1)
+        harm = total * norm * beam_rows_t[None]
+        harm_ref[:, :, t * wide : (t + 1) * wide] = harm
         squares = jnp.sum(harm * harm, axis=(0, 1)) * (1.0 / orders)
-        power[t : t + 1] = squares.reshape(1, LANES)
+        power[:, t * wide : (t + 1) * wide] = squares.reshape(1, wide)
 
     for step in range(chunks + 3):
         if step < chunks:
             multiply(step)
         if 1 <= step <= chunks:
             to_plane(step - 1)
-        if step == 2:
-            beam_rows()
         if 2 <= step <= chunks + 1:
             to_z(step - 2)
         if 3 <= step:
@@ -321,8 +337,12 @@
     for d in range(1, ma_n):
         scopies[d - 1].wait()
         spectrum = spectrum + precv_power[d - 1]
-    for t in range(chunks):
-        spec_ref[:, t * LANES : (t + 1) * LANES] = spectrum[t : t + 1]
+    spec_ref[...] = spectrum
+
+
+def hand_on(harm_in, spec_in, harm_out, spec_out):
+    harm_out[...] = harm_in[...]
+    spec_out[...] = spec_in[...]
 
 
 def per_device(blk_n, ma_n, sky_map, legendre, m_list, block_start, beam_ratio):
@@ -330,17 +350,17 @@
     cycles, orders, degrees = legendre.shape
     own_n = m_list.shape[1]
     share = degrees // blk_n
-    chunks = share // LANES
+    chunks = CHUNKS
+    wide = share // chunks
     planes = blk_n // 2
     period = 2 * orders
     q_all = npix // period
     pieces = 4
-    dims = (blk_n, ma_n, cycles, orders, own_n, degrees, npix, pieces)
+    dims = (blk_n, ma_n, cycles, orders, own_n, degrees, npix, pieces, chunks)
     beam = beam_ratio.reshape(-1, LANES)
     f32, bf16 = jnp.float32, jnp.bfloat16
     dma = pltpu.SemaphoreType.DMA
     vmem = pl.BlockSpec(memory_space=pltpu.VMEM)
-    smem = pl.BlockSpec(memory_space=pltpu.SMEM)
     anywhere = pl.BlockSpec(memory_space=pl.ANY)
     harm, spec = pl.pallas_call(
         functools.partial(kernel, dims),
@@ -348,26 +368,30 @@
             jax.ShapeDtypeStruct((2, own_n, share), f32),
             jax.ShapeDtypeStruct((1, share), f32),
         ),
-        in_specs=[anywhere, anywhere, smem, smem, vmem],
+        in_specs=[anywhere] * 5,
         out_specs=(vmem, vmem),
         scratch_shapes=[
+            pltpu.SMEM(m_list.shape, jnp.int32),
+            pltpu.SMEM(block_start.shape, jnp.int32),
+            pltpu.VMEM(beam.shape, f32),
             pltpu.VMEM(sky_map.shape, f32),
             pltpu.VMEM(legendre.shape, bf16),
             pltpu.VMEM((2, 16, 8, period), f32),
             pltpu.VMEM((2, q_all // 16, 8, period), f32),
             pltpu.VMEM((4 * orders, cycles * orders), bf16),
-            pltpu.VMEM((chunks, planes, 2 * orders, LANES), bf16),
-            pltpu.VMEM((chunks, planes, 2 * orders, LANES), f32),
-            pltpu.VMEM((chunks, planes, 2 * orders, LANES), bf16),
-            pltpu.VMEM((chunks, planes - 1, 2 * orders, LANES), bf16),
-            pltpu.VMEM((chunks, planes - 1, 2 * orders, LANES), bf16),
-            pltpu.VMEM((chunks, 2, ma_n, own_n, LANES), f32),
-            pltpu.VMEM((chunks, ma_n - 1, 2, own_n, LANES), bf16),
-            pltpu.VMEM((chunks, ma_n - 1, 2, own_n, LANES), bf16),
-            pltpu.VMEM((chunks, own_n, LANES), f32),
+            pltpu.VMEM((chunks, planes, 2 * orders, wide), bf16),
+            pltpu.VMEM((chunks, planes, 2 * orders, wide), f32),
+            pltpu.VMEM((chunks, planes, 2 * orders, wide), bf16),
+            pltpu.VMEM((chunks, planes - 1, 2 * orders, wide), bf16),
+            pltpu.VMEM((chunks, planes - 1, 2 * orders, wide), bf16),
+            pltpu.VMEM((chunks, 2, ma_n, own_n, wide), f32),
+            pltpu.VMEM((chunks, ma_n - 1, 2, own_n, wide), bf16),
+            pltpu.VMEM((chunks, ma_n - 1, 2, own_n, wide), bf16),
+            pltpu.VMEM((share // LANES, own_n, LANES), f32),
             pltpu.VMEM((2 * beam.shape[0], LANES), f32),
-            pltpu.VMEM((chunks, LANES), f32),
-            pltpu.VMEM((ma_n - 1, chunks, LANES), f32),
+            pltpu.VMEM((1, share), f32),
+            pltpu.VMEM((ma_n - 1, 1, share), f32),
+            dma((3,)),
             dma((pieces,)),
             dma,
             dma((2, chunks)),
@@ -379,6 +403,12 @@
             collective_id=0, has_side_effects=True, vmem_limit_bytes=56 * 1024 * 1024
         ),
     )(sky_map, legendre, m_list, block_start, beam)
+    harm, spec = pl.pallas_call(
+        hand_on,
+        out_shape=(jax.ShapeDtypeStruct(harm.shape, f32), jax.ShapeDtypeStruct(spec.shape, f32)),
+        in_specs=[vmem] * 2,
+        out_specs=(vmem, vmem),
+    )(harm, spec)
     return harm, spec.reshape(share)
 
 

time: 33.1 us -> 26.9 us (0.81)
  Pallas kernels: 29.5 us -> 26.1 us
  local copies, waits for them, and re-layouts: 2.72 us -> 0 us
    pallas_call x1, Pallas kernels: 29.5 us -> 24.6 us  [per_device(): pl.pallas_call(functools.partial(kernel, dims), out_shape=(jax.ShapeDtype...]
    unnamed x2 -> x0, local copies, waits for them, and re-layouts: 2.72 us -> none
    pallas_call x0 -> x1, Pallas kernels: none -> 1.48 us  [per_device(): pl.pallas_call(hand_on, out_shape=(jax.ShapeDtypeStruct(harm.shape, f32),...]
where the time goes in v2:
time: 26.9 us; the launch traced here: 26.8 us
  Pallas kernels  26.1 us (97%)
  between operations  0.64 us (2%)
    pallas_call x1, Pallas kernels, per_device(): pl.pallas_call(functools.partial(kernel, dims), out_shape=(jax.ShapeDtype...  24.6 us
    pallas_call x1, Pallas kernels, per_device(): pl.pallas_call(hand_on, out_shape=(jax.ShapeDtypeStruct(harm.shape, f32),...  1.48 us

profile of v2, /device:TPU:0, one launch (start us, length us, event | category | flops | bytes accessed | tf_op | source)
XLA Modules:
  0.0 26.8 jit_solution(10176266086253554805)
XLA Ops:
  0.6 24.6 %shard_map.68 = (f32[2,16,512]{2,1,0:T(8,128)}, f32[1,512]{1,0:T(1,128)}) custom-call(f32[2,8,65536]{2,1,0:T(8,128)} %sky_hbm.1, bf16[8,64,4096]{2,1,0:T(8,128)(2,1)} %leg_hbm.1, s32[4,16]{1,0:T(4,128)} %m_hbm.1, s32[64,64]{1,0:T(8,128)} %block_hbm.1, f32[256,128]{1,0:T(8,128)} %bitcast.2), custom_call_target="tpu_custom_call" | custom-call | tf_op jit(solution)/shard_map/pallas_call | solution.py:365
  25.3 1.5 %shard_map.69 = (f32[2,16,512]{2,1,0:T(8,128)}, f32[1,512]{1,0:T(1,128)}) custom-call(f32[2,16,512]{2,1,0:T(8,128)} %get-tuple-element.6.harm_in, f32[1,512]{1,0:T(1,128)} %get-tuple-element.7.spec_in), custom_call_target="tpu_custom_call" | custom-call | tf_op jit(solution)/shard_map/pallas_call | solution.py:406

commit v3 on v2

--- a/solution.py
+++ b/solution.py
@@ -39,6 +39,7 @@
     beam_hbm,
     harm_ref,
     spec_ref,
+    harm_vmem,
     m_ref,
     block_ref,
     beam_ref,
@@ -60,6 +61,7 @@
     power,
     precv_power,
     small_sem,
+    out_sem,
     sky_sem,
     leg_sem,
     psem,
@@ -159,10 +161,6 @@
             return carry
 
         lax.fori_loop(0, own_n, one, 0)
-
-    block_copy.wait()
-    beam_copy.wait()
-    beam_rows()
 
     zero = jnp.zeros((cycles, period), jnp.float32)
 
@@ -301,7 +299,7 @@
         tiles = wide // LANES
         beam_rows_t = jnp.concatenate([ratio[t * tiles + i] for i in range(tiles)], axis=1)
         harm = total * norm * beam_rows_t[None]
-        harm_ref[:, :, t * wide : (t + 1) * wide] = harm
+        harm_vmem[:, :, t * wide : (t + 1) * wide] = harm
         squares = jnp.sum(harm * harm, axis=(0, 1)) * (1.0 / orders)
         power[:, t * wide : (t + 1) * wide] = squares.reshape(1, wide)
 
@@ -310,6 +308,10 @@
             multiply(step)
         if 1 <= step <= chunks:
             to_plane(step - 1)
+        if step == 2:
+            block_copy.wait()
+            beam_copy.wait()
+            beam_rows()
         if 2 <= step <= chunks + 1:
             to_z(step - 2)
         if 3 <= step:
@@ -327,6 +329,8 @@
         )
         copy.start()
         scopies.append(copy)
+    out_copy = pltpu.make_async_copy(harm_vmem, harm_ref, out_sem)
+    out_copy.start()
     for t in range(chunks):
         pcopies[t].wait_send()
         for d in range(1, planes):
@@ -338,6 +342,7 @@
         scopies[d - 1].wait()
         spectrum = spectrum + precv_power[d - 1]
     spec_ref[...] = spectrum
+    out_copy.wait()
 
 
 def hand_on(harm_in, spec_in, harm_out, spec_out):
@@ -369,8 +374,9 @@
             jax.ShapeDtypeStruct((1, share), f32),
         ),
         in_specs=[anywhere] * 5,
-        out_specs=(vmem, vmem),
+        out_specs=(anywhere, vmem),
         scratch_shapes=[
+            pltpu.VMEM((2, own_n, share), f32),
             pltpu.SMEM(m_list.shape, jnp.int32),
             pltpu.SMEM(block_start.shape, jnp.int32),
             pltpu.VMEM(beam.shape, f32),
@@ -392,6 +398,7 @@
             pltpu.VMEM((1, share), f32),
             pltpu.VMEM((ma_n - 1, 1, share), f32),
             dma((3,)),
+            dma,
             dma((pieces,)),
             dma,
             dma((2, chunks)),

time: 26.9 us -> 26.1 us (0.970)
  Pallas kernels: 26.1 us -> 25.3 us
    pallas_call x1, Pallas kernels: 24.6 us -> 23.8 us  [per_device(): pl.pallas_call(functools.partial(kernel, dims), out_shape=(jax.ShapeDtype...]
where the time goes in v3:
time: 26.1 us; the launch traced here: 25.9 us
  Pallas kernels  25.3 us (97%)
  between operations  0.64 us (2%)
    pallas_call x1, Pallas kernels, per_device(): pl.pallas_call(functools.partial(kernel, dims), out_shape=(jax.ShapeDtype...  23.8 us
    pallas_call x1, Pallas kernels, per_device(): pl.pallas_call(hand_on, out_shape=(jax.ShapeDtypeStruct(harm.shape, f32),...  1.48 us

profile of v3, /device:TPU:0, one launch (start us, length us, event | category | flops | bytes accessed | tf_op | source)
XLA Modules:
  0.0 25.9 jit_solution(5031471454460372172)
XLA Ops:
  0.6 23.8 %shard_map.68 = (f32[2,16,512]{2,1,0:T(8,128)}, f32[1,512]{1,0:T(1,128)}) custom-call(f32[2,8,65536]{2,1,0:T(8,128)} %sky_hbm.1, bf16[8,64,4096]{2,1,0:T(8,128)(2,1)} %leg_hbm.1, s32[4,16]{1,0:T(4,128)} %m_hbm.1, s32[64,64]{1,0:T(8,128)} %block_hbm.1, f32[256,128]{1,0:T(8,128)} %bitcast.2), custom_call_target="tpu_custom_call" | custom-call | tf_op jit(solution)/shard_map/pallas_call | solution.py:370
  24.5 1.5 %shard_map.69 = (f32[2,16,512]{2,1,0:T(8,128)}, f32[1,512]{1,0:T(1,128)}) custom-call(f32[2,16,512]{2,1,0:T(8,128)} %get-tuple-element.6.harm_in, f32[1,512]{1,0:T(1,128)} %get-tuple-element.7.spec_in), custom_call_target="tpu_custom_call" | custom-call | tf_op jit(solution)/shard_map/pallas_call | solution.py:413
